TPU v7x, 512 devices: a whole 4x8x8 slice. The times are simulated.
512 devices in a mesh: rep: 4 (over z_lo), fsdp: 16 (over y, core), tp: 8 (over z_hi, x).
Axes of the slice: x: 4, y: 8, z: 8 (z_hi: 2, z_lo: 4; z = z_hi * 4 + z_lo), core: 2. Of those that a mesh axis runs over, the one named last changes fastest.
Arguments:
- delta_attn: float32 [4, 4, 768, 768], P('rep', None, 'fsdp', 'tp'), may hold values from -4 to 4
- delta_in: float32 [4, 768, 3072], P('rep', 'fsdp', 'tp'), may hold values from -4 to 4
- delta_out: float32 [4, 3072, 768], P('rep', 'fsdp', 'tp'), may hold values from -4 to 4
- delta_small: float32 [4, 1920], P('rep'), may hold values from -4 to 4
- emb_left: float32 [4, 8, 4016, 64], P('rep', 'tp', 'fsdp'), may hold values from -6 to 6
- emb_right: float32 [4, 64, 768], P('rep'), may hold values from -0.75 to 0.75
- anchor_attn: float32 [8, 294912], P('tp', 'fsdp'), may hold values from -6 to 6
- anchor_in: float32 [8, 294912], P('tp', 'fsdp'), may hold values from -6 to 6
- anchor_out: float32 [8, 294912], P('tp', 'fsdp'), may hold values from -6 to 6
- anchor_small: float32 [1920], P('fsdp'), may hold values from -6 to 6
- anchor_emb: float32 [8, 16, 4, 48192], P('tp', 'fsdp', 'rep'), may hold values from -6 to 6
- moment_attn: float32 [8, 294912], P('tp', 'fsdp'), may hold values from -4 to 4
- moment_in: float32 [8, 294912], P('tp', 'fsdp'), may hold values from -4 to 4
- moment_out: float32 [8, 294912], P('tp', 'fsdp'), may hold values from -4 to 4
- moment_small: float32 [1920], P('fsdp'), may hold values from -4 to 4
- moment_emb: float32 [8, 16, 4, 48192], P('tp', 'fsdp', 'rep'), may hold values from -4 to 4
Outputs:
- new_attn: float32 [4, 768, 768], P(None, 'fsdp', 'tp')
- new_in: float32 [768, 3072], P('fsdp', 'tp')
- new_out: float32 [3072, 768], P('fsdp', 'tp')
- new_small: float32 [1920], replicated
- new_emb: float32 [32128, 768], P('tp', 'fsdp')
- next_attn: float32 [8, 294912], P('tp', 'fsdp')
- next_in: float32 [8, 294912], P('tp', 'fsdp')
- next_out: float32 [8, 294912], P('tp', 'fsdp')
- next_small: float32 [1920], P('fsdp')
- next_emb: float32 [8, 16, 4, 48192], P('tp', 'fsdp', 'rep')
All inputs are finite; a program needn't handle non-finite values.
Results may differ from a plain program's by a relative error of at most 0.000071.
Values sent between devices are 32-bit elements; how exact they have to be, the bound alone decides.
A program may use at most 64 MiB of HBM per device.

v0:
```python
import jax
import jax.numpy as jnp
from jax import lax
from jax.sharding import PartitionSpec as P

OUTER_RATE = 0.7
MOMENTUM_COEF = 0.9


def nesterov(anchor, moment, mean_delta):
    moment_next = MOMENTUM_COEF * moment + mean_delta
    updated = anchor - OUTER_RATE * (mean_delta + MOMENTUM_COEF * moment_next)
    return (updated, moment_next)


def to_blocks(matrix, lead, shards):
    local_rows = matrix.shape[-2]
    width = matrix.shape[-1] // shards
    shaped = matrix.reshape(lead, local_rows, shards, width)
    return jnp.transpose(shaped, (2, 3, 0, 1))


def from_blocks(blocks):
    shards, width, lead, local_rows = blocks.shape
    return jnp.transpose(blocks, (2, 3, 0, 1)).reshape(lead, local_rows, shards * width)


def on_device(
    delta_attn,
    delta_in,
    delta_out,
    delta_small,
    emb_left,
    emb_right,
    anchor_attn,
    anchor_in,
    anchor_out,
    anchor_small,
    anchor_emb,
    moment_attn,
    moment_in,
    moment_out,
    moment_small,
    moment_emb,
):
    groups = lax.axis_size("rep")
    shards = lax.axis_size("fsdp")
    send_attn = to_blocks(delta_attn[0], 4, shards)
    send_in = to_blocks(delta_in[0][None], 1, shards)
    send_out = to_blocks(delta_out[0][None], 1, shards)
    flat_attn, flat_in, flat_out = (
        lax.all_to_all(send_attn, "fsdp", split_axis=0, concat_axis=3, tiled=True),
        lax.all_to_all(send_in, "fsdp", split_axis=0, concat_axis=3, tiled=True),
        lax.all_to_all(send_out, "fsdp", split_axis=0, concat_axis=3, tiled=True),
    )
    block_shapes = (flat_attn.shape, flat_in.shape, flat_out.shape)
    portion = anchor_small.shape[0]
    small_local = lax.dynamic_slice_in_dim(
        delta_small[0], lax.axis_index("fsdp") * portion, portion, 0
    )[None, :]
    differences = (
        flat_attn.reshape(flat_attn.shape[1] * flat_attn.shape[2], flat_attn.shape[3]),
        flat_in.reshape(flat_in.shape[1], flat_in.shape[3]),
        flat_out.reshape(flat_out.shape[1], flat_out.shape[3]),
        small_local,
    )
    anchors = (
        anchor_attn.reshape(differences[0].shape),
        anchor_in.reshape(differences[1].shape),
        anchor_out.reshape(differences[2].shape),
        anchor_small[None, :],
    )
    moments = (
        moment_attn.reshape(differences[0].shape),
        moment_in.reshape(differences[1].shape),
        moment_out.reshape(differences[2].shape),
        moment_small[None, :],
    )
    totals = lax.psum((differences[0], differences[1], differences[2], differences[3]), "rep")
    updated_list = []
    moment_list = []
    for summed, anchor_part, moment_part in zip(totals, anchors, moments):
        updated, moment_next = nesterov(anchor_part, moment_part, summed / groups)
        updated_list.append(updated)
        moment_list.append(moment_next)
    back_attn = updated_list[0].reshape(block_shapes[0])
    back_in = updated_list[1].reshape(block_shapes[1])
    back_out = updated_list[2].reshape(block_shapes[2])
    train_attn, train_in, train_out = (
        lax.all_to_all(back_attn, "fsdp", split_axis=3, concat_axis=0, tiled=True),
        lax.all_to_all(back_in, "fsdp", split_axis=3, concat_axis=0, tiled=True),
        lax.all_to_all(back_out, "fsdp", split_axis=3, concat_axis=0, tiled=True),
    )
    new_attn = from_blocks(train_attn)
    new_in = from_blocks(train_in)[0]
    new_out = from_blocks(train_out)[0]
    new_small = lax.all_gather(updated_list[3].reshape(portion), "fsdp", axis=0, tiled=True)
    left_local = emb_left[0, 0]
    right_local = emb_right[0]
    block_rows = left_local.shape[0]
    column_count = right_local.shape[1] // groups
    product_term = jnp.dot(
        left_local, right_local, precision=lax.Precision.HIGHEST, preferred_element_type=jnp.float32
    )
    summed_emb = lax.psum_scatter(product_term, "rep", scatter_dimension=1, tiled=True)
    anchor_rows = anchor_emb[0, 0, 0].reshape(block_rows, column_count)
    moment_rows = moment_emb[0, 0, 0].reshape(block_rows, column_count)
    new_emb_part, next_emb_part = nesterov(anchor_rows, moment_rows, summed_emb / groups)
    full_rows = lax.all_gather(new_emb_part, "rep", axis=1, tiled=True)
    new_emb = lax.all_to_all(full_rows, "fsdp", split_axis=1, concat_axis=0, tiled=True)
    return (
        new_attn,
        new_in,
        new_out,
        new_small,
        new_emb,
        moment_list[0].reshape(moment_attn.shape),
        moment_list[1].reshape(moment_in.shape),
        moment_list[2].reshape(moment_out.shape),
        moment_list[3].reshape(moment_small.shape),
        next_emb_part.reshape(moment_emb.shape),
    )


def solution(mesh):
    placed = (
        P("rep", None, "fsdp", "tp"),
        P("rep", "fsdp", "tp"),
        P("rep", "fsdp", "tp"),
        P("rep", None),
        P("rep", "tp", "fsdp", None),
        P("rep", None, None),
        P("tp", "fsdp"),
        P("tp", "fsdp"),
        P("tp", "fsdp"),
        P("fsdp"),
        P("tp", "fsdp", "rep", None),
        P("tp", "fsdp"),
        P("tp", "fsdp"),
        P("tp", "fsdp"),
        P("fsdp"),
        P("tp", "fsdp", "rep", None),
    )
    return jax.shard_map(
        on_device,
        mesh=mesh,
        in_specs=placed,
        out_specs=(
            P(None, "fsdp", "tp"),
            P("fsdp", "tp"),
            P("fsdp", "tp"),
            P(),
            P("tp", "fsdp"),
            P("tp", "fsdp"),
            P("tp", "fsdp"),
            P("tp", "fsdp"),
            P("fsdp"),
            P("tp", "fsdp", "rep", None),
        ),
        check_vma=False,
    )
```

profile of v0, /device:TPU:32, one launch (start us, length us, event | category | flops | bytes accessed | tf_op | source)
XLA Modules:
  0.0 245.8 jit_solution(11660199578842059813)
XLA Ops:
  9.1 8.8 %all-to-all-start.2 = ((f32[16,1,1152]{2,1,0:T(1,128)}), f32[16,1,1152]{2,1,0:T(1,128)S(1)}, u32[]{:S(2)}, u32[]{:S(2)}) async-start(f32[16,1,1152]{2,1,0:T(1,128)} %reshape.155), calls=%async_computation.2 | async-start | bytes 147456 | tf_op jit(solution)/shard_map/all_to_all | solution.py:53
  19.8 1.4 all-to-all-done.2
  21.2 8.2 %all-to-all-start = ((f32[16,1,1152]{2,1,0:T(1,128)}), f32[16,1,1152]{2,1,0:T(1,128)S(1)}, u32[]{:S(2)}, u32[]{:S(2)}) async-start(f32[16,1,1152]{2,1,0:T(1,128)} %reshape.151), calls=%async_computation | async-start | bytes 147456 | tf_op jit(solution)/shard_map/all_to_all | solution.py:52
  29.3 1.6 copy.94
  32.6 8.2 %all-to-all-start.4 = ((f32[16,6,1,192]{3,2,1,0:T(1,128)}), f32[16,6,1,192]{3,2,1,0:T(1,128)S(1)}, u32[]{:S(2)}, u32[]{:S(2)}) async-start(f32[16,6,1,192]{3,2,1,0:T(1,128)} %bitcast.21), calls=%async_computation.4 | async-start | bytes 196608 | tf_op jit(solution)/shard_map/all_to_all | solution.py:54
  45.6 1.7 fusion
  55.9 48.3 %all-reduce.4.cloned.1.call-done = (f32[24,768]{1,0:T(8,128)}, f32[24,768]{1,0:T(8,128)}, f32[6,3072]{1,0:T(8,128)}) async-done(((f32[24,768]{1,0:T(8,128)}, f32[24,768]{1,0:T(8,128)}, f32[6,3072]{1,0:T(8,128)}), (f32[24,768]{1,0:T(8,128)}, f32[24,768]{1,0:T(8,128)}, f32[6,3072]{1,0:T(8,128)})) %all-reduce.4.cloned.1.call-update) | async-done | bytes 221200 | tf_op jit(solution)/shard_map/psum | solution.py:79
  104.1 1.6 fusion.2
  105.7 1.6 copy.96
  107.3 13.7 %reduce.32 = f32[3072,6]{1,0:T(8,128)S(1)} reduce(f32[3072,1,1,6]{3,2,1,0:T(1,128)S(1)} %bitcast.106, f32[]{:T(128)} %broadcast.90), dimensions={1,2}, to_apply=%bitcast.99.reduce_sub_computation | reduce | bytes 147460
  121.1 1.9 reshape.159
  123.0 7.2 %all-to-all-start.5 = ((f32[16,1,1152]{2,1,0:T(1,128)}), f32[16,1,1152]{2,1,0:T(1,128)S(1)}, u32[]{:S(2)}, u32[]{:S(2)}) async-start(f32[16,1,1152]{2,1,0:T(1,128)} %reshape.159), calls=%async_computation.5 | async-start | bytes 147456 | tf_op jit(solution)/shard_map/all_to_all | solution.py:92
  131.2 1.6 reduce.30
  135.1 2.5 %reshape.153 = f32[16,1,1152]{2,1,0:T(1,128)} reshape(f32[768,1,4,6]{3,2,1,0:T(4,128)S(1)} %bitcast.103) | data formatting | bytes 147456
  137.6 7.2 %all-to-all-start.3 = ((f32[16,1,1152]{2,1,0:T(1,128)}), f32[16,1,1152]{2,1,0:T(1,128)S(1)}, u32[]{:S(2)}, u32[]{:S(2)}) async-start(f32[16,1,1152]{2,1,0:T(1,128)} %reshape.157), calls=%async_computation.3 | async-start | bytes 147456 | tf_op jit(solution)/shard_map/all_to_all | solution.py:91
  145.9 2.2 all-to-all-done.3
  148.1 8.1 %all-to-all-start.1 = ((f32[16,1,1152]{2,1,0:T(1,128)}), f32[16,1,1152]{2,1,0:T(1,128)S(1)}, u32[]{:S(2)}, u32[]{:S(2)}) async-start(f32[16,1,1152]{2,1,0:T(1,128)} %reshape.153), calls=%async_computation.1 | async-start | bytes 147456 | tf_op jit(solution)/shard_map/all_to_all | solution.py:90
  156.3 18.3 %all_gather.7 = f32[251,768]{0,1:T(8,128)} all-gather(f32[251,192]{0,1:T(8,128)S(1)} %get-tuple-element.54), channel_id=1, replica_groups=mesh['rep'=4,'fsdp'=16,'tp'=8] {'rep'}, dimensions={1}, use_global_device_ids=true | all-gather | bytes 963840 | tf_op jit(solution)/shard_map/all_gather | solution.py:109
  174.6 7.2 %all-to-all-start.6 = ((f32[251,16,48]{0,2,1:T(8,128)}), f32[251,16,48]{0,2,1:T(8,128)S(1)}, u32[]{:S(2)}, u32[]{:S(2)}) async-start(f32[251,16,48]{0,2,1:T(8,128)} %bitcast.35), calls=%async_computation.7 | async-start | bytes 1572864 | tf_op jit(solution)/shard_map/all_to_all | solution.py:110
  184.5 10.2 %psum.31 = f32[1,120]{1,0:T(1,128)S(1)} all-reduce(f32[1,120]{1,0:T(1,128)S(1)} %constant_dynamic-slice_fusion), channel_id=1, replica_groups=mesh['rep'=4,'fsdp'=16,'tp'=8] {'rep'}, use_global_device_ids=true, to_apply=%region_3.0 | all-reduce | flops 120 | bytes 960 | tf_op jit(solution)/shard_map/psum | solution.py:79
  194.8 26.9 %all-reduce = f32[1920]{0:T(1024)} all-reduce(f32[1920]{0:T(1024)S(1)} %bitcast_dynamic-update-slice_fusion), channel_id=2, replica_groups=mesh['rep'=4,'fsdp'=16,'tp'=8] {'fsdp'}, use_global_device_ids=true, to_apply=%add | all-reduce | flops 1920 | bytes 15360 | tf_op jit(solution)/shard_map/all_gather | solution.py:97
  225.2 2.5 reshape.160
  232.5 2.0 reshape.154
  237.7 1.3 all_to_all.110
  (124 shorter events, 36.4 us)
Async XLA Ops:
  7.2 38.4 %copy-start = (f32[1,64,768]{2,1,0:T(8,128)S(1)}, f32[1,64,768]{2,1,0:T(8,128)}, u32[]{:S(2)}) copy-start(f32[1,64,768]{2,1,0:T(8,128)} %param.21) | copy-start | bytes 589828
  9.1 12.1 %all-to-all-start.2 = ((f32[16,1,1152]{2,1,0:T(1,128)}), f32[16,1,1152]{2,1,0:T(1,128)S(1)}, u32[]{:S(2)}, u32[]{:S(2)}) async-start(f32[16,1,1152]{2,1,0:T(1,128)} %reshape.155), calls=%async_computation.2 | async-start | bytes 147456 | tf_op jit(solution)/shard_map/all_to_all | solution.py:53
  21.2 11.4 %all-to-all-start = ((f32[16,1,1152]{2,1,0:T(1,128)}), f32[16,1,1152]{2,1,0:T(1,128)S(1)}, u32[]{:S(2)}, u32[]{:S(2)}) async-start(f32[16,1,1152]{2,1,0:T(1,128)} %reshape.151), calls=%async_computation | async-start | bytes 147456 | tf_op jit(solution)/shard_map/all_to_all | solution.py:52
  32.3 13.3 %copy-start.21 = (f32[1,1,251,64]{2,3,1,0:T(8,128)S(1)}, f32[1,1,251,64]{2,3,1,0:T(8,128)}, u32[]{:S(2)}) copy-start(f32[1,1,251,64]{2,3,1,0:T(8,128)} %param.20) | copy-start | bytes 192772
  32.6 12.0 %all-to-all-start.4 = ((f32[16,6,1,192]{3,2,1,0:T(1,128)}), f32[16,6,1,192]{3,2,1,0:T(1,128)S(1)}, u32[]{:S(2)}, u32[]{:S(2)}) async-start(f32[16,6,1,192]{3,2,1,0:T(1,128)} %bitcast.21), calls=%async_computation.4 | async-start | bytes 196608 | tf_op jit(solution)/shard_map/all_to_all | solution.py:54
  40.8 63.4 %all-reduce.4.cloned.1.call-start = ((), (), s32[]{:S(2)}) async-start(), calls=%async_computation.9 | async-start | bytes 491520 | tf_op jit(solution)/shard_map/psum | solution.py:79
  45.4 99.5 %reduce-scatter.2.cloned.1.call-start = ((), (), s32[]{:S(2)}) async-start(), calls=%async_computation.8 | async-start | bytes 983040 | tf_op jit(solution)/shard_map/reduce_scatter | solution.py:105
  121.0 9.2 %copy-start.9 = (f32[24,768]{1,0:T(8,128)S(1)}, f32[24,768]{1,0:T(8,128)}, u32[]{:S(2)}) copy-start(f32[24,768]{1,0:T(8,128)} %reshape.92) | copy-start | bytes 221188
  121.0 9.2 %copy-start.10 = (f32[24,768]{1,0:T(8,128)S(1)}, f32[24,768]{1,0:T(8,128)}, u32[]{:S(2)}) copy-start(f32[24,768]{1,0:T(8,128)} %mul.77) | copy-start | bytes 221188
  121.0 9.2 %copy-start.20 = (f32[24,768]{1,0:T(8,128)S(1)}, f32[24,768]{1,0:T(8,128)}, u32[]{:S(2)}) copy-start(f32[24,768]{1,0:T(8,128)} %get-tuple-element.51) | copy-start | bytes 221188
  121.0 12.7 %copy-start.7 = (f32[24,768]{1,0:T(8,128)S(1)}, f32[24,768]{1,0:T(8,128)}, u32[]{:S(2)}) copy-start(f32[24,768]{1,0:T(8,128)} %reshape.88) | copy-start | bytes 221188
  121.0 12.7 %copy-start.8 = (f32[24,768]{1,0:T(8,128)S(1)}, f32[24,768]{1,0:T(8,128)}, u32[]{:S(2)}) copy-start(f32[24,768]{1,0:T(8,128)} %mul.73) | copy-start | bytes 221188
  121.0 12.7 %copy-start.19 = (f32[24,768]{1,0:T(8,128)S(1)}, f32[24,768]{1,0:T(8,128)}, u32[]{:S(2)}) copy-start(f32[24,768]{1,0:T(8,128)} %get-tuple-element.50) | copy-start | bytes 221188
  123.0 14.6 %all-to-all-start.5 = ((f32[16,1,1152]{2,1,0:T(1,128)}), f32[16,1,1152]{2,1,0:T(1,128)S(1)}, u32[]{:S(2)}, u32[]{:S(2)}) async-start(f32[16,1,1152]{2,1,0:T(1,128)} %reshape.159), calls=%async_computation.5 | async-start | bytes 147456 | tf_op jit(solution)/shard_map/all_to_all | solution.py:92
  134.4 10.5 %copy-start.1 = (f32[251,192]{0,1:T(8,128)S(1)}, f32[251,192]{0,1:T(8,128)}, u32[]{:S(2)}) copy-start(f32[251,192]{0,1:T(8,128)} %copy.99) | copy-start | bytes 578308
  137.6 10.5 %all-to-all-start.3 = ((f32[16,1,1152]{2,1,0:T(1,128)}), f32[16,1,1152]{2,1,0:T(1,128)S(1)}, u32[]{:S(2)}, u32[]{:S(2)}) async-start(f32[16,1,1152]{2,1,0:T(1,128)} %reshape.157), calls=%async_computation.3 | async-start | bytes 147456 | tf_op jit(solution)/shard_map/all_to_all | solution.py:91
  145.8 48.8 %copy-start.22 = (f32[120]{0:T(128)S(1)}, f32[120]{0:T(128)}, u32[]{:S(2)}) copy-start(f32[120]{0:T(128)} %param.25) | copy-start | bytes 1444
  145.9 48.8 %copy-start.23 = (f32[120]{0:T(128)S(1)}, f32[120]{0:T(128)}, u32[]{:S(2)}) copy-start(f32[120]{0:T(128)} %param.30) | copy-start | bytes 1444
  145.9 76.3 %copy-start.2 = (f32[1,1,6,3072]{3,2,1,0:T(8,128)S(1)}, f32[1,1,6,3072]{3,2,1,0:T(8,128)}, u32[]{:S(2)}) copy-start(f32[1,1,6,3072]{3,2,1,0:T(8,128)} %get-tuple-element.55) | copy-start | bytes 221188
  145.9 77.0 %copy-start.5 = (f32[1,1,24,768]{3,2,1,0:T(8,128)S(1)}, f32[1,1,24,768]{3,2,1,0:T(8,128)}, u32[]{:S(2)}) copy-start(f32[1,1,24,768]{3,2,1,0:T(8,128)} %get-tuple-element.57) | copy-start | bytes 221188
  145.9 77.7 %copy-start.6 = (f32[1,1,24,768]{3,2,1,0:T(8,128)S(1)}, f32[1,1,24,768]{3,2,1,0:T(8,128)}, u32[]{:S(2)}) copy-start(f32[1,1,24,768]{3,2,1,0:T(8,128)} %get-tuple-element.59) | copy-start | bytes 221188
  148.1 76.2 %copy-start.3 = (f32[16,1,1152]{2,1,0:T(1,128)}, f32[16,1,1152]{2,1,0:T(1,128)S(1)}, u32[]{:S(2)}) copy-start(f32[16,1,1152]{2,1,0:T(1,128)S(1)} %all-to-all-done.3) | copy-start | bytes 221188
  148.1 26.4 %all-to-all-start.1 = ((f32[16,1,1152]{2,1,0:T(1,128)}), f32[16,1,1152]{2,1,0:T(1,128)S(1)}, u32[]{:S(2)}, u32[]{:S(2)}) async-start(f32[16,1,1152]{2,1,0:T(1,128)} %reshape.153), calls=%async_computation.1 | async-start | bytes 147456 | tf_op jit(solution)/shard_map/all_to_all | solution.py:90
  174.6 62.6 %all-to-all-start.6 = ((f32[251,16,48]{0,2,1:T(8,128)}), f32[251,16,48]{0,2,1:T(8,128)S(1)}, u32[]{:S(2)}, u32[]{:S(2)}) async-start(f32[251,16,48]{0,2,1:T(8,128)} %bitcast.35), calls=%async_computation.7 | async-start | bytes 1572864 | tf_op jit(solution)/shard_map/all_to_all | solution.py:110
  (9 other events, 52.3 us)
Sparse Core Ops, SparseCore 0:
  45.5 58.6 all-reduce.3
  107.8 30.1 reduce-scatter.1
where the time goes:
time: 247 us; the launch traced here: 246 us
  blocking collectives  55.4 us (22%)
  starting transfers between devices  55.2 us (22%)
  waiting for transfers between devices  53.1 us (21%)
  local copies, waits for them, and re-layouts  37.2 us (15%)
  other arithmetic  27.9 us (11%)
  between operations  15.3 us (6%)
    psum x1, waiting for transfers between devices, on_device(): lax.psum((differences[0], differences[1], differences[2], differences[3])...  48.3 us
    all_gather x1, blocking collectives, on_device(): lax.all_gather(updated_list[3].reshape(portion), 'fsdp', axis=0, tiled=True)  26.9 us
    unnamed x70, local copies, waits for them, and re-layouts  22.5 us
    unnamed x10, other arithmetic  21.2 us
    all_gather x1, blocking collectives, on_device(): full_rows = lax.all_gather(new_emb_part, 'rep', axis=1, tiled=True)  18.3 us
    psum x1, blocking collectives, on_device(): lax.psum((differences[0], differences[1], differences[2], differences[3])...  10.2 us
    all_to_all x1, starting transfers between devices, on_device(): lax.all_to_all(send_in, 'fsdp', split_axis=0, concat_axis=3, tiled=True)  8.82 us
    all_to_all x1, starting transfers between devices, on_device(): lax.all_to_all(send_out, 'fsdp', split_axis=0, concat_axis=3, tiled=True)  8.17 us
  transfers between devices with their start and end apart: 9, of which 5 were waited for; matrix products, arithmetic and copies ran while one was open for 25% of the time, Pallas kernels for 0%

commit v1 on v0

--- a/solution.py
+++ b/solution.py
@@ -1,10 +1,22 @@
+import functools
 import jax
 import jax.numpy as jnp
 from jax import lax
 from jax.sharding import PartitionSpec as P
+from jax.lax import all_to_all, axis_size
 
 OUTER_RATE = 0.7
 MOMENTUM_COEF = 0.9
+
+
+def see_shards_by_axis(raw, group_axis, which_dim):
+    g_now = jnp.concatenate(
+        all_to_all(jnp.stack([raw] * axis_size(group_axis)), group_axis, 0, 0), axis=which_dim
+    )
+    return g_now
+
+
+list_region = functools.partial(see_shards_by_axis, group_axis="fsdp", which_dim=0)
 
 
 def nesterov(anchor, moment, mean_delta):
@@ -94,7 +106,7 @@
     new_attn = from_blocks(train_attn)
     new_in = from_blocks(train_in)[0]
     new_out = from_blocks(train_out)[0]
-    new_small = lax.all_gather(updated_list[3].reshape(portion), "fsdp", axis=0, tiled=True)
+    new_small = list_region(updated_list[3].reshape(portion))
     left_local = emb_left[0, 0]
     right_local = emb_right[0]
     block_rows = left_local.shape[0]

time: 247 us -> 217 us (0.88)
  the two profiles are of different devices: /device:TPU:32 before, /device:TPU:1 now
where the time goes in v1:
time: 217 us; the launch traced here: 216 us
  waiting for transfers between devices  59.1 us (27%)
  starting transfers between devices  48.3 us (22%)
  local copies, waits for them, and re-layouts  36 us (17%)
  other arithmetic  29 us (13%)
  blocking collectives  26.9 us (12%)
  between operations  14.6 us (7%)
    psum x1, waiting for transfers between devices, on_device(): lax.psum((differences[0], differences[1], differences[2], differences[3])...  24.9 us
    unnamed x9, other arithmetic  21.7 us
    unnamed x60, local copies, waits for them, and re-layouts  21.2 us
    all_gather x1, blocking collectives, on_device(): full_rows = lax.all_gather(new_emb_part, 'rep', axis=1, tiled=True)  16.2 us
    psum x1, blocking collectives, on_device(): lax.psum((differences[0], differences[1], differences[2], differences[3])...  10.7 us
    all_to_all x1, starting transfers between devices, on_device(): lax.all_to_all(send_in, 'fsdp', split_axis=0, concat_axis=3, tiled=True)  10.2 us
    all_to_all x1, starting transfers between devices, on_device(): lax.all_to_all(back_out, 'fsdp', split_axis=3, concat_axis=0, tiled=True)  9.62 us
    all_to_all x1, starting transfers between devices, on_device(): lax.all_to_all(full_rows, 'fsdp', split_axis=1, concat_axis=0, tiled=True)  9.32 us
  transfers between devices with their start and end apart: 10, of which 7 were waited for; matrix products, arithmetic and copies ran while one was open for 29% of the time, Pallas kernels for 0%

profile of v1, /device:TPU:1, one launch (start us, length us, event | category | flops | bytes accessed | tf_op | source)
XLA Modules:
  0.0 215.7 jit_solution(9350186677892509709)
XLA Ops:
  9.1 10.2 %all-to-all-start.2 = ((f32[16,1,1152]{2,1,0:T(1,128)}), f32[16,1,1152]{2,1,0:T(1,128)S(1)}, u32[]{:S(2)}, u32[]{:S(2)}) async-start(f32[16,1,1152]{2,1,0:T(1,128)} %reshape.163), calls=%async_computation.2 | async-start | bytes 147456 | tf_op jit(solution)/shard_map/all_to_all | solution.py:65
  21.1 6.1 %all-to-all-done.2 = f32[16,1,1152]{2,1,0:T(1,128)S(1)} async-done(((f32[16,1,1152]{2,1,0:T(1,128)}), f32[16,1,1152]{2,1,0:T(1,128)S(1)}, u32[]{:S(2)}, u32[]{:S(2)}) %all-to-all-start.2) | async-done | bytes 73760 | tf_op jit(solution)/shard_map/all_to_all | solution.py:65
  27.3 3.4 %all-to-all-start = ((f32[16,1,1152]{2,1,0:T(1,128)}), f32[16,1,1152]{2,1,0:T(1,128)S(1)}, u32[]{:S(2)}, u32[]{:S(2)}) async-start(f32[16,1,1152]{2,1,0:T(1,128)} %reshape.159), calls=%async_computation | async-start | bytes 147456 | tf_op jit(solution)/shard_map/all_to_all | solution.py:64
  30.7 1.6 copy.94
  33.8 4.9 %all-to-all-done = f32[16,1,1152]{2,1,0:T(1,128)S(1)} async-done(((f32[16,1,1152]{2,1,0:T(1,128)}), f32[16,1,1152]{2,1,0:T(1,128)S(1)}, u32[]{:S(2)}, u32[]{:S(2)}) %all-to-all-start) | async-done | bytes 73760 | tf_op jit(solution)/shard_map/all_to_all | solution.py:64
  38.7 3.4 %all-to-all-start.4 = ((f32[16,6,1,192]{3,2,1,0:T(1,128)}), f32[16,6,1,192]{3,2,1,0:T(1,128)S(1)}, u32[]{:S(2)}, u32[]{:S(2)}) async-start(f32[16,6,1,192]{3,2,1,0:T(1,128)} %bitcast.21), calls=%async_computation.4 | async-start | bytes 196608 | tf_op jit(solution)/shard_map/all_to_all | solution.py:66
  44.9 5.8 %all-to-all-done.4 = f32[16,6,1,192]{3,2,1,0:T(1,128)S(1)} async-done(((f32[16,6,1,192]{3,2,1,0:T(1,128)}), f32[16,6,1,192]{3,2,1,0:T(1,128)S(1)}, u32[]{:S(2)}, u32[]{:S(2)}) %all-to-all-start.4) | async-done | bytes 73760 | tf_op jit(solution)/shard_map/all_to_all | solution.py:66
  51.5 1.7 fusion
  54.1 10.7 %psum.31 = f32[1,120]{1,0:T(1,128)S(1)} all-reduce(f32[1,120]{1,0:T(1,128)S(1)} %constant_dynamic-slice_fusion), channel_id=1, replica_groups=mesh['rep'=4,'fsdp'=16,'tp'=8] {'rep'}, use_global_device_ids=true, to_apply=%region_3.0 | all-reduce | flops 120 | bytes 960 | tf_op jit(solution)/shard_map/psum | solution.py:91
  65.9 5.5 %all-to-all-start.6 = ((f32[16,1,120]{2,1,0:T(1,128)}), f32[16,1,120]{2,1,0:T(1,128)S(1)}, u32[]{:S(2)}, u32[]{:S(2)}) async-start(f32[16,1,120]{2,1,0:T(1,128)} %stack.3), calls=%async_computation.6 | async-start | bytes 16384 | tf_op jit(solution)/shard_map/all_to_all | solution.py:14
  78.3 24.9 %all-reduce.3.cloned.1.call-done = (f32[24,768]{1,0:T(8,128)}, f32[24,768]{1,0:T(8,128)}, f32[6,3072]{1,0:T(8,128)}) async-done(((f32[24,768]{1,0:T(8,128)}, f32[24,768]{1,0:T(8,128)}, f32[6,3072]{1,0:T(8,128)}), (f32[24,768]{1,0:T(8,128)}, f32[24,768]{1,0:T(8,128)}, f32[6,3072]{1,0:T(8,128)})) %all-reduce.3.cloned.1.call-update) | async-done | bytes 221200 | tf_op jit(solution)/shard_map/psum | solution.py:91
  107.9 13.7 %reduce.36 = f32[3072,6]{1,0:T(8,128)S(1)} reduce(f32[3072,1,1,6]{3,2,1,0:T(1,128)S(1)} %bitcast.105, f32[]{:T(128)} %broadcast.98), dimensions={1,2}, to_apply=%bitcast.98.reduce_sub_computation | reduce | bytes 147460
  121.6 1.9 reshape.167
  126.3 9.6 %all-to-all-start.5 = ((f32[16,1,1152]{2,1,0:T(1,128)}), f32[16,1,1152]{2,1,0:T(1,128)S(1)}, u32[]{:S(2)}, u32[]{:S(2)}) async-start(f32[16,1,1152]{2,1,0:T(1,128)} %reshape.167), calls=%async_computation.5 | async-start | bytes 147456 | tf_op jit(solution)/shard_map/all_to_all | solution.py:104
  137.4 2.5 %reshape.161 = f32[16,1,1152]{2,1,0:T(1,128)} reshape(f32[768,1,4,6]{3,2,1,0:T(4,128)S(1)} %bitcast.102) | data formatting | bytes 147456
  139.9 4.1 %all-to-all-done.5 = f32[16,1,1152]{2,1,0:T(1,128)S(1)} async-done(((f32[16,1,1152]{2,1,0:T(1,128)}), f32[16,1,1152]{2,1,0:T(1,128)S(1)}, u32[]{:S(2)}, u32[]{:S(2)}) %all-to-all-start.5) | async-done | bytes 73760 | tf_op jit(solution)/shard_map/all_to_all | solution.py:104
  143.9 3.4 %all-to-all-start.3 = ((f32[16,1,1152]{2,1,0:T(1,128)}), f32[16,1,1152]{2,1,0:T(1,128)S(1)}, u32[]{:S(2)}, u32[]{:S(2)}) async-start(f32[16,1,1152]{2,1,0:T(1,128)} %reshape.165), calls=%async_computation.3 | async-start | bytes 147456 | tf_op jit(solution)/shard_map/all_to_all | solution.py:103
  148.4 7.0 %all-to-all-done.3 = f32[16,1,1152]{2,1,0:T(1,128)S(1)} async-done(((f32[16,1,1152]{2,1,0:T(1,128)}), f32[16,1,1152]{2,1,0:T(1,128)S(1)}, u32[]{:S(2)}, u32[]{:S(2)}) %all-to-all-start.3) | async-done | bytes 73760 | tf_op jit(solution)/shard_map/all_to_all | solution.py:103
  155.4 3.4 %all-to-all-start.1 = ((f32[16,1,1152]{2,1,0:T(1,128)}), f32[16,1,1152]{2,1,0:T(1,128)S(1)}, u32[]{:S(2)}, u32[]{:S(2)}) async-start(f32[16,1,1152]{2,1,0:T(1,128)} %reshape.161), calls=%async_computation.1 | async-start | bytes 147456 | tf_op jit(solution)/shard_map/all_to_all | solution.py:102
  158.8 16.2 %all_gather.3 = f32[251,768]{0,1:T(8,128)} all-gather(f32[251,192]{0,1:T(8,128)S(1)} %get-tuple-element.54), channel_id=1, replica_groups=mesh['rep'=4,'fsdp'=16,'tp'=8] {'rep'}, dimensions={1}, use_global_device_ids=true | all-gather | bytes 963840 | tf_op jit(solution)/shard_map/all_gather | solution.py:121
  175.0 9.3 %all-to-all-start.7 = ((f32[251,16,48]{0,2,1:T(8,128)}), f32[251,16,48]{0,2,1:T(8,128)S(1)}, u32[]{:S(2)}, u32[]{:S(2)}) async-start(f32[251,16,48]{0,2,1:T(8,128)} %bitcast.34), calls=%async_computation.8 | async-start | bytes 1572864 | tf_op jit(solution)/shard_map/all_to_all | solution.py:122
  188.6 2.5 %reshape.168 = f32[3072,1,1,6]{3,2,1,0:T(1,128)S(1)} reshape(f32[16,1152]{1,0:T(8,128)S(1)} %reduce.37) | data formatting | bytes 147456
  195.8 2.0 reshape.162
  200.6 6.4 %all-to-all-done.7 = f32[251,16,48]{0,2,1:T(8,128)S(1)} async-done(((f32[251,16,48]{0,2,1:T(8,128)}), f32[251,16,48]{0,2,1:T(8,128)S(1)}, u32[]{:S(2)}, u32[]{:S(2)}) %all-to-all-start.7) | async-done | bytes 771104 | tf_op jit(solution)/shard_map/all_to_all | solution.py:122
  (117 shorter events, 40.9 us)
Async XLA Ops:
  7.2 44.3 %copy-start = (f32[1,64,768]{2,1,0:T(8,128)S(1)}, f32[1,64,768]{2,1,0:T(8,128)}, u32[]{:S(2)}) copy-start(f32[1,64,768]{2,1,0:T(8,128)} %param.21) | copy-start | bytes 589828
  9.1 18.2 %all-to-all-start.2 = ((f32[16,1,1152]{2,1,0:T(1,128)}), f32[16,1,1152]{2,1,0:T(1,128)S(1)}, u32[]{:S(2)}, u32[]{:S(2)}) async-start(f32[16,1,1152]{2,1,0:T(1,128)} %reshape.163), calls=%async_computation.2 | async-start | bytes 147456 | tf_op jit(solution)/shard_map/all_to_all | solution.py:65
  27.3 11.4 %all-to-all-start = ((f32[16,1,1152]{2,1,0:T(1,128)}), f32[16,1,1152]{2,1,0:T(1,128)S(1)}, u32[]{:S(2)}, u32[]{:S(2)}) async-start(f32[16,1,1152]{2,1,0:T(1,128)} %reshape.159), calls=%async_computation | async-start | bytes 147456 | tf_op jit(solution)/shard_map/all_to_all | solution.py:64
  33.7 17.8 %copy-start.17 = (f32[1,1,251,64]{2,3,1,0:T(8,128)S(1)}, f32[1,1,251,64]{2,3,1,0:T(8,128)}, u32[]{:S(2)}) copy-start(f32[1,1,251,64]{2,3,1,0:T(8,128)} %param.20) | copy-start | bytes 192772
  38.7 11.9 %all-to-all-start.4 = ((f32[16,6,1,192]{3,2,1,0:T(1,128)}), f32[16,6,1,192]{3,2,1,0:T(1,128)S(1)}, u32[]{:S(2)}, u32[]{:S(2)}) async-start(f32[16,6,1,192]{3,2,1,0:T(1,128)} %bitcast.21), calls=%async_computation.4 | async-start | bytes 196608 | tf_op jit(solution)/shard_map/all_to_all | solution.py:66
  42.1 61.0 %all-reduce.3.cloned.1.call-start = ((), (), s32[]{:S(2)}) async-start(), calls=%async_computation.10 | async-start | bytes 491520 | tf_op jit(solution)/shard_map/psum | solution.py:91
  44.0 20.7 %copy-start.18 = (f32[120]{0:T(128)S(1)}, f32[120]{0:T(128)}, u32[]{:S(2)}) copy-start(f32[120]{0:T(128)} %param.30) | copy-start | bytes 1444
  44.0 20.7 %copy-start.19 = (f32[120]{0:T(128)S(1)}, f32[120]{0:T(128)}, u32[]{:S(2)}) copy-start(f32[120]{0:T(128)} %param.25) | copy-start | bytes 1444
  44.0 27.8 %copy-start.10 = (f32[1,18432]{1,0:T(1,128)S(1)}, f32[1,18432]{1,0:T(1,128)}, u32[]{:S(2)}) copy-start(f32[1,18432]{1,0:T(1,128)} %param.24) | copy-start | bytes 221188
  44.1 28.5 %copy-start.14 = (f32[1,18432]{1,0:T(1,128)S(1)}, f32[1,18432]{1,0:T(1,128)}, u32[]{:S(2)}) copy-start(f32[1,18432]{1,0:T(1,128)} %param.29) | copy-start | bytes 221188
  44.1 28.5 %copy-start.15 = (f32[1,18432]{1,0:T(1,128)S(1)}, f32[1,18432]{1,0:T(1,128)}, u32[]{:S(2)}) copy-start(f32[1,18432]{1,0:T(1,128)} %param.28) | copy-start | bytes 221188
  50.6 22.4 %copy-start.11 = (f32[1,18432]{1,0:T(1,128)S(1)}, f32[1,18432]{1,0:T(1,128)}, u32[]{:S(2)}) copy-start(f32[1,18432]{1,0:T(1,128)} %param.23) | copy-start | bytes 221188
  51.4 22.4 %copy-start.12 = (f32[1,18432]{1,0:T(1,128)S(1)}, f32[1,18432]{1,0:T(1,128)}, u32[]{:S(2)}) copy-start(f32[1,18432]{1,0:T(1,128)} %param.22) | copy-start | bytes 221188
  51.4 23.8 %copy-start.13 = (f32[1,18432]{1,0:T(1,128)S(1)}, f32[1,18432]{1,0:T(1,128)}, u32[]{:S(2)}) copy-start(f32[1,18432]{1,0:T(1,128)} %param.27) | copy-start | bytes 221188
  51.4 95.9 %reduce-scatter.2.cloned.1.call-start = ((), (), s32[]{:S(2)}) async-start(), calls=%async_computation.9 | async-start | bytes 983040 | tf_op jit(solution)/shard_map/reduce_scatter | solution.py:117
  53.2 22.9 %copy-start.8 = (f32[1,1,1,48192]{3,2,1,0:T(1,128)S(1)}, f32[1,1,1,48192]{3,2,1,0:T(1,128)}, u32[]{:S(2)}) copy-start(f32[1,1,1,48192]{3,2,1,0:T(1,128)} %param.26) | copy-start | bytes 578308
  65.9 60.5 %all-to-all-start.6 = ((f32[16,1,120]{2,1,0:T(1,128)}), f32[16,1,120]{2,1,0:T(1,128)S(1)}, u32[]{:S(2)}, u32[]{:S(2)}) async-start(f32[16,1,120]{2,1,0:T(1,128)} %stack.3), calls=%async_computation.6 | async-start | bytes 16384 | tf_op jit(solution)/shard_map/all_to_all | solution.py:14
  126.3 17.6 %all-to-all-start.5 = ((f32[16,1,1152]{2,1,0:T(1,128)}), f32[16,1,1152]{2,1,0:T(1,128)S(1)}, u32[]{:S(2)}, u32[]{:S(2)}) async-start(f32[16,1,1152]{2,1,0:T(1,128)} %reshape.167), calls=%async_computation.5 | async-start | bytes 147456 | tf_op jit(solution)/shard_map/all_to_all | solution.py:104
  143.9 11.4 %all-to-all-start.3 = ((f32[16,1,1152]{2,1,0:T(1,128)}), f32[16,1,1152]{2,1,0:T(1,128)S(1)}, u32[]{:S(2)}, u32[]{:S(2)}) async-start(f32[16,1,1152]{2,1,0:T(1,128)} %reshape.165), calls=%async_computation.3 | async-start | bytes 147456 | tf_op jit(solution)/shard_map/all_to_all | solution.py:103
  148.4 37.2 %copy-start.2 = (f32[1,1,6,3072]{3,2,1,0:T(8,128)S(1)}, f32[1,1,6,3072]{3,2,1,0:T(8,128)}, u32[]{:S(2)}) copy-start(f32[1,1,6,3072]{3,2,1,0:T(8,128)} %get-tuple-element.55) | copy-start | bytes 221188
  148.4 37.9 %copy-start.4 = (f32[1,1,24,768]{3,2,1,0:T(8,128)S(1)}, f32[1,1,24,768]{3,2,1,0:T(8,128)}, u32[]{:S(2)}) copy-start(f32[1,1,24,768]{3,2,1,0:T(8,128)} %get-tuple-element.57) | copy-start | bytes 221188
  148.4 38.6 %copy-start.5 = (f32[1,1,24,768]{3,2,1,0:T(8,128)S(1)}, f32[1,1,24,768]{3,2,1,0:T(8,128)}, u32[]{:S(2)}) copy-start(f32[1,1,24,768]{3,2,1,0:T(8,128)} %get-tuple-element.59) | copy-start | bytes 221188
  155.4 19.7 %all-to-all-start.1 = ((f32[16,1,1152]{2,1,0:T(1,128)}), f32[16,1,1152]{2,1,0:T(1,128)S(1)}, u32[]{:S(2)}, u32[]{:S(2)}) async-start(f32[16,1,1152]{2,1,0:T(1,128)} %reshape.161), calls=%async_computation.1 | async-start | bytes 147456 | tf_op jit(solution)/shard_map/all_to_all | solution.py:102
  175.0 32.0 %all-to-all-start.7 = ((f32[251,16,48]{0,2,1:T(8,128)}), f32[251,16,48]{0,2,1:T(8,128)S(1)}, u32[]{:S(2)}, u32[]{:S(2)}) async-start(f32[251,16,48]{0,2,1:T(8,128)} %bitcast.34), calls=%async_computation.8 | async-start | bytes 1572864 | tf_op jit(solution)/shard_map/all_to_all | solution.py:122
  (6 other events, 66.8 us)
Sparse Core Ops, SparseCore 0:
  51.5 51.5 all-reduce.2
  106.8 31.1 reduce-scatter.1
